TPU v7x, 32 devices: a whole 2x2x4 slice. The times are simulated.
32 devices in a mesh: had: 4 (over z), blk: 8 (over y, x, core).
Axes of the slice: x: 2, y: 2, z: 4, core: 2. Of those that a mesh axis runs over, the one named last changes fastest.
Arguments:
- panel: bfloat16 [65536, 512], P(('had', 'blk')), may hold values from -100 to 100
- signs: int32 [65536], P(('had', 'blk')), may hold values from 0 to 1
- sample_rows: int32 [8, 2048], P('blk'), may hold values from 0 to 8191
Outputs:
- q_panel: bfloat16 [65536, 512], P(('had', 'blk'))
- r_sketch: float32 [512, 512], replicated
- r_gram: float32 [512, 512], replicated
All inputs are finite; a program needn't handle non-finite values.
Results may differ from a plain program's by a relative error of at most 0.0075.
The roundings to bfloat16 on the way count: a program that leaves them out, or rounds other values in their place, can miss the bound.
Values sent between devices are 32-bit elements; how exact they have to be, the bound alone decides.
A program may use at most 448 MiB of HBM per device.

v0:
```python
import math
import jax
import jax.numpy as jnp
from jax import lax
from jax.sharding import PartitionSpec as P

LH = 32


def bit_parity(value):
    counted = jnp.zeros_like(value)
    for shift_count in range(16):
        counted = counted + jnp.bitwise_and(jnp.right_shift(value, shift_count), 1)
    return counted % 2


def hadamard(order):
    first = lax.broadcasted_iota(jnp.int32, (order, order), 0)
    second = lax.broadcasted_iota(jnp.int32, (order, order), 1)
    parity = bit_parity(jnp.bitwise_and(first, second))
    return (1 - 2 * parity).astype(jnp.float32)


def upper_factor(matrix):
    return jnp.linalg.cholesky(matrix).T


def lower_inverse(lower):
    order = lower.shape[0]
    inverse = (1.0 / jnp.diagonal(lower)).reshape(order, 1, 1)
    width = 1
    while width < order:
        count = order // (2 * width)
        tiles = lower.reshape(count, 2 * width, count, 2 * width)
        diag_tiles = jnp.moveaxis(jnp.diagonal(tiles, axis1=0, axis2=2), -1, 0)
        corner = diag_tiles[:, width:, :width]
        first_inv = inverse[0::2]
        second_inv = inverse[1::2]
        partial_value = jnp.einsum(
            "ajk,akl->ajl", corner, first_inv, precision=lax.Precision.HIGHEST
        )
        lower_left = -jnp.einsum(
            "aij,ajl->ail", second_inv, partial_value, precision=lax.Precision.HIGHEST
        )
        zero_tile = jnp.zeros_like(corner)
        top_half = jnp.concatenate([first_inv, zero_tile], axis=2)
        bottom_half = jnp.concatenate([lower_left, second_inv], axis=2)
        inverse = jnp.concatenate([top_half, bottom_half], axis=1)
        width = width * 2
    return inverse[0]


def inverse_upper(factor):
    return lower_inverse(factor.T).T


def on_device(panel, signs, sample_rows):
    n_had = lax.axis_size("had")
    n_blk = lax.axis_size("blk")
    my_group = lax.axis_index("had")
    rows_dev, columns = panel.shape
    sketch_count = sample_rows.shape[1]
    groups = rows_dev // LH
    flipped = jnp.where(signs[:, None] == 1, -panel, panel)
    inner = hadamard(LH).astype(jnp.bfloat16)
    mixed = jnp.einsum(
        "ml,glk->gmk",
        inner,
        flipped.reshape(groups, LH, columns),
        preferred_element_type=jnp.float32,
    )
    mixed = mixed.reshape(rows_dev, columns)
    picks = sample_rows[0]
    owners = picks // rows_dev
    offsets = picks % rows_dev
    factor = 1.0 / math.sqrt(n_had * LH * sketch_count * n_blk)
    parity = bit_parity(jnp.bitwise_and(owners, my_group))
    weights = (1 - 2 * parity).astype(jnp.float32) * factor
    partial_sketch = jnp.take(mixed, offsets, axis=0) * weights[:, None]
    sketch = lax.psum(partial_sketch, ("had", "blk"))
    sketch_gram = jnp.dot(
        sketch.T, sketch, precision=lax.Precision.HIGHEST, preferred_element_type=jnp.float32
    )
    r_sketch = upper_factor(sketch_gram)
    sketch_inverse = inverse_upper(r_sketch).astype(jnp.bfloat16)
    whitened = jnp.dot(panel, sketch_inverse, preferred_element_type=jnp.float32).astype(
        jnp.bfloat16
    )
    partial_gram = jnp.einsum("rk,rj->kj", whitened, whitened, preferred_element_type=jnp.float32)
    summed = lax.psum(partial_gram, ("had", "blk"))
    gram_matrix = summed / (rows_dev * n_had * n_blk)
    r_gram = upper_factor(gram_matrix)
    gram_inverse = inverse_upper(r_gram).astype(jnp.bfloat16)
    q_panel = jnp.dot(whitened, gram_inverse, preferred_element_type=jnp.float32).astype(
        jnp.bfloat16
    )
    return (q_panel, r_sketch, r_gram)


def solution(mesh):
    placed = (P(("had", "blk"), None), P(("had", "blk")), P("blk", None))
    return jax.shard_map(
        on_device,
        mesh=mesh,
        in_specs=placed,
        out_specs=(P(("had", "blk"), None), P(), P()),
        check_vma=False,
    )
```

profile of v0, /device:TPU:0, one launch (start us, length us, event | category | flops | bytes accessed | tf_op | source)
XLA Modules:
  0.0 1226.9 jit_solution(7551053319992622696)
XLA Ops:
  12.5 11.7 gather_fusion
  28.4 145.2 %all-reduce.22.cloned.1.call-done = f32[2048,512]{1,0:T(8,128)} async-done(((f32[2048,512]{1,0:T(8,128)}), f32[2048,512]{1,0:T(8,128)}) %all-reduce.22.cloned.1.call-update) | async-done | bytes 4194320 | tf_op jit(solution)/shard_map/psum | solution.py:80
  185.7 11.7 cholesky.286
  209.9 11.7 cholesky.305
  233.4 11.7 cholesky.326
  256.4 11.7 cholesky.343
  278.0 68.4 %reshape.325 = f32[256,2,256,2]{3,2,1,0:T(8,128)} reshape(f32[512,512]{1,0:T(8,128)S(1)} %select_select_fusion.1) | data formatting | bytes 2097152 | tf_op jit(solution)/shard_map/reshape | solution.py:34
  346.4 35.9 %reshape.326 = f32[128,4,128,4]{3,2,1,0:T(8,128)} reshape(f32[512,512]{1,0:T(8,128)S(1)} %select_select_fusion.1) | data formatting | bytes 2097152 | tf_op jit(solution)/shard_map/reshape | solution.py:34
  406.7 107.3 %copy.213 = f32[256,2,256,2]{3,1,2,0:T(2,128)} copy(f32[256,2,256,2]{3,2,1,0:T(8,128)} %reshape.325) | data formatting | bytes 2097152 | tf_op jit(solution)/shard_map/reshape | solution.py:34
  517.3 38.0 %copy.215 = f32[128,4,128,4]{3,1,2,0:T(4,128)} copy(f32[128,4,128,4]{3,2,1,0:T(8,128)} %reshape.326) | data formatting | bytes 2097152 | tf_op jit(solution)/shard_map/reshape | solution.py:34
  559.5 20.5 %copy.217 = f32[64,8,64,8]{3,1,2,0:T(8,128)} copy(f32[64,8,64,8]{3,2,1,0:T(8,128)} %reshape.327) | data formatting | bytes 2097152 | tf_op jit(solution)/shard_map/reshape | solution.py:34
  587.8 14.2 %copy.219 = f32[32,16,32,16]{3,1,2,0:T(8,128)} copy(f32[32,16,32,16]{3,2,1,0:T(8,128)} %reshape.328) | data formatting | bytes 2097152 | tf_op jit(solution)/shard_map/reshape | solution.py:34
  637.0 128.6 %all-reduce.24.cloned.1.call-done = f32[512,512]{0,1:T(8,128)} async-done(((f32[512,512]{0,1:T(8,128)}), f32[512,512]{0,1:T(8,128)}) %all-reduce.24.cloned.1.call-update) | async-done | bytes 1048592 | tf_op jit(solution)/shard_map/psum | solution.py:90
  767.7 11.7 cholesky.358
  790.2 11.7 cholesky.377
  812.5 11.7 cholesky.398
  835.1 11.7 cholesky.415
  857.2 68.4 %reshape.336 = f32[256,2,256,2]{3,2,1,0:T(8,128)} reshape(f32[512,512]{1,0:T(8,128)S(1)} %select_select_fusion) | data formatting | bytes 2097152 | tf_op jit(solution)/shard_map/reshape | solution.py:34
  925.6 35.9 %reshape.337 = f32[128,4,128,4]{3,2,1,0:T(8,128)} reshape(f32[512,512]{1,0:T(8,128)S(1)} %select_select_fusion) | data formatting | bytes 2097152 | tf_op jit(solution)/shard_map/reshape | solution.py:34
  961.5 11.0 reshape.338
  986.3 107.3 %copy.212 = f32[256,2,256,2]{3,1,2,0:T(2,128)} copy(f32[256,2,256,2]{3,2,1,0:T(8,128)} %reshape.336) | data formatting | bytes 2097152 | tf_op jit(solution)/shard_map/reshape | solution.py:34
  1096.9 37.8 %copy.214 = f32[128,4,128,4]{3,1,2,0:T(4,128)} copy(f32[128,4,128,4]{3,2,1,0:T(8,128)} %reshape.337) | data formatting | bytes 2097152 | tf_op jit(solution)/shard_map/reshape | solution.py:34
  1138.9 20.3 %copy.216 = f32[64,8,64,8]{3,1,2,0:T(8,128)} copy(f32[64,8,64,8]{3,2,1,0:T(8,128)} %reshape.338) | data formatting | bytes 2097152 | tf_op jit(solution)/shard_map/reshape | solution.py:34
  1167.0 14.2 %copy.218 = f32[32,16,32,16]{3,1,2,0:T(8,128)} copy(f32[32,16,32,16]{3,2,1,0:T(8,128)} %reshape.339) | data formatting | bytes 2097152 | tf_op jit(solution)/shard_map/reshape | solution.py:34
  (244 shorter events, 247.6 us)
Async XLA Ops:
  7.2 166.4 %all-reduce.22.cloned.1.call-start = ((), (), s32[]{:S(2)}) async-start(), calls=%async_computation | async-start | bytes 8388608 | tf_op jit(solution)/shard_map/psum | solution.py:80
  9.7 2.7 copy-start.22
  28.2 737.5 %all-reduce.24.cloned.1.call-start = ((), (), s32[]{:S(2)}) async-start(), calls=%async_computation.1 | async-start | bytes 2097152 | tf_op jit(solution)/shard_map/psum | solution.py:90
  28.2 527.1 %copy-start.4 = (s32[128]{0:T(128)}, s32[128]{0:T(128)S(1)}, u32[]{:S(2)}) copy-start(s32[128]{0:T(128)S(1)} %or_bitcast_fusion.6) | copy-start | bytes 1540
  28.3 551.8 %copy-start.6 = (s32[64]{0:T(128)}, s32[64]{0:T(128)S(1)}, u32[]{:S(2)}) copy-start(s32[64]{0:T(128)S(1)} %or_bitcast_fusion.5) | copy-start | bytes 772
  28.3 573.7 %copy-start.15 = (s32[32]{0:T(128)}, s32[32]{0:T(128)S(1)}, u32[]{:S(2)}) copy-start(s32[32]{0:T(128)S(1)} %or_bitcast_fusion.4) | copy-start | bytes 388
  28.3 583.9 %copy-start.17 = (s32[16]{0:T(128)}, s32[16]{0:T(128)S(1)}, u32[]{:S(2)}) copy-start(s32[16]{0:T(128)S(1)} %or_bitcast_fusion.3) | copy-start | bytes 196
  28.3 590.8 %copy-start.20 = (s32[8]{0:T(128)}, s32[8]{0:T(128)S(1)}, u32[]{:S(2)}) copy-start(s32[8]{0:T(128)S(1)} %or_bitcast_fusion.2) | copy-start | bytes 100
  28.4 595.0 %copy-start.23 = (s32[4]{0:T(128)}, s32[4]{0:T(128)S(1)}, u32[]{:S(2)}) copy-start(s32[4]{0:T(128)S(1)} %or_bitcast_fusion.1) | copy-start | bytes 52
  28.4 485.6 %copy-start.2 = (s32[256,1]{0,1:T(1,128)}, s32[256,1]{0,1:T(1,128)S(1)}, u32[]{:S(2)}) copy-start(s32[256,1]{0,1:T(1,128)S(1)} %shift-left_or_fusion.1) | copy-start | bytes 3076
  28.4 244.4 %copy-start = (s32[512,1]{0,1:T(1,128)}, s32[512,1]{0,1:T(1,128)S(1)}, u32[]{:S(2)}) copy-start(s32[512,1]{0,1:T(1,128)S(1)} %shift-left_or_fusion) | copy-start | bytes 6148
  184.7 1.0 copy-start.10
  632.0 1.3 copy-start.25
  765.7 1.8 copy-start.8
  767.7 84.6 %copy-start.1 = (s32[512,1]{0,1:T(1,128)S(1)}, s32[512,1]{0,1:T(1,128)}, u32[]{:S(2)}) copy-start(s32[512,1]{0,1:T(1,128)} %copy-done) | copy-start | bytes 6148
  986.3 107.3 %copy-start.3 = (s32[256,1]{0,1:T(1,128)S(1)}, s32[256,1]{0,1:T(1,128)}, u32[]{:S(2)}) copy-start(s32[256,1]{0,1:T(1,128)} %copy-done.2) | copy-start | bytes 3076
  1096.9 37.8 %copy-start.5 = (s32[128]{0:T(128)S(1)}, s32[128]{0:T(128)}, u32[]{:S(2)}) copy-start(s32[128]{0:T(128)} %copy-done.4) | copy-start | bytes 1540
  1138.9 20.3 %copy-start.7 = (s32[64]{0:T(128)S(1)}, s32[64]{0:T(128)}, u32[]{:S(2)}) copy-start(s32[64]{0:T(128)} %copy-done.6) | copy-start | bytes 772
  1167.0 14.2 %copy-start.16 = (s32[32]{0:T(128)S(1)}, s32[32]{0:T(128)}, u32[]{:S(2)}) copy-start(s32[32]{0:T(128)} %copy-done.15) | copy-start | bytes 388
  1186.0 5.4 copy-start.18
  1191.5 7.0 copy-start.21
  1198.5 6.7 copy-start.24
  1205.1 5.3 copy-start.9
  1210.6 1.7 copy-start.19
  (4 other events, 3.1 us)
Sparse Core Ops, SparseCore 0:
  28.3 145.2 all-reduce.21
  635.7 129.9 all-reduce.23
where the time goes:
time: 1230 us
  local copies, waits for them, and re-layouts  708 us (58%)
  waiting for transfers between devices  274 us (22%)
  other arithmetic  175 us (14%)
  matrix products  49 us (4%)
  between operations  21 us (2%)
    reshape x32, local copies, waits for them, and re-layouts, lower_inverse(): tiles = lower.reshape(count, 2 * width, count, 2 * width)  635 us
    another operation x29, other arithmetic, upper_factor(): return jnp.linalg.cholesky(matrix).T  158 us
    psum x1, waiting for transfers between devices, on_device(): sketch = lax.psum(partial_sketch, ('had', 'blk'))  145 us
    psum x1, waiting for transfers between devices, on_device(): summed = lax.psum(partial_gram, ('had', 'blk'))  129 us
    gather x16, local copies, waits for them, and re-layouts, lower_inverse(): diag_tiles = jnp.moveaxis(jnp.diagonal(tiles, axis1=0, axis2=2), -1, 0)  40.2 us
  transfers between devices with their start and end apart: 2, of which 2 were waited for; matrix products, arithmetic and copies ran while one was open for 0% of the time, Pallas kernels for 0%

commit v1 on v0

--- a/solution.py
+++ b/solution.py
@@ -77,7 +77,7 @@
     parity = bit_parity(jnp.bitwise_and(owners, my_group))
     weights = (1 - 2 * parity).astype(jnp.float32) * factor
     partial_sketch = jnp.take(mixed, offsets, axis=0) * weights[:, None]
-    sketch = lax.psum(partial_sketch, ("had", "blk"))
+    sketch = jnp.sum(lax.all_gather(partial_sketch, ("had", "blk")), axis=0)
     sketch_gram = jnp.dot(
         sketch.T, sketch, precision=lax.Precision.HIGHEST, preferred_element_type=jnp.float32
     )

time: 1230 us -> 1810 us (1.47)
  waiting for transfers between devices: 274 us -> 805 us
  other arithmetic: 175 us -> 221 us
    all_gather x0 -> x1, waiting for transfers between devices: none -> 678 us  [on_device(): sketch = jnp.sum(lax.all_gather(partial_sketch, ('had', 'blk')), axis=0)]
    psum x1 -> x0, waiting for transfers between devices: 145 us -> none  [on_device(): sketch = lax.psum(partial_sketch, ('had', 'blk'))]
    reduce_sum x0 -> x1, other arithmetic: none -> 42.8 us  [on_device(): sketch = jnp.sum(lax.all_gather(partial_sketch, ('had', 'blk')), axis=0)]
where the time goes in v1:
time: 1810 us; the launch traced here: 1800 us
  waiting for transfers between devices  805 us (44%)
  local copies, waits for them, and re-layouts  708 us (39%)
  other arithmetic  221 us (12%)
  matrix products  49.2 us (3%)
  between operations  20.9 us (1%)
    all_gather x1, waiting for transfers between devices, on_device(): sketch = jnp.sum(lax.all_gather(partial_sketch, ('had', 'blk')), axis=0)  678 us
    reshape x32, local copies, waits for them, and re-layouts, lower_inverse(): tiles = lower.reshape(count, 2 * width, count, 2 * width)  635 us
    another operation x29, other arithmetic, upper_factor(): return jnp.linalg.cholesky(matrix).T  158 us
    psum x1, waiting for transfers between devices, on_device(): summed = lax.psum(partial_gram, ('had', 'blk'))  128 us
    reduce_sum x1, other arithmetic, on_device(): sketch = jnp.sum(lax.all_gather(partial_sketch, ('had', 'blk')), axis=0)  42.8 us
    gather x16, local copies, waits for them, and re-layouts, lower_inverse(): diag_tiles = jnp.moveaxis(jnp.diagonal(tiles, axis1=0, axis2=2), -1, 0)  40.3 us
  transfers between devices with their start and end apart: 2, of which 2 were waited for; matrix products, arithmetic and copies ran while one was open for 0% of the time, Pallas kernels for 0%

profile of v1, /device:TPU:0, one launch (start us, length us, event | category | flops | bytes accessed | tf_op | source)
XLA Modules:
  0.0 1804.3 jit_solution(6527619167056811034)
XLA Ops:
  12.5 11.7 gather_fusion
  31.5 677.6 %all-gather.2.cloned.1.call-done = f32[32,2048,512]{2,1,0:T(8,128)} async-done(((f32[1,2048,512]{2,1,0:T(8,128)}), f32[32,2048,512]{2,1,0:T(8,128)}) %all-gather.2.cloned.1.call-update) | async-done | bytes 134217744 | tf_op jit(solution)/shard_map/all_gather | solution.py:80
  709.1 42.8 %reduce_sum.9 = f32[2048,512]{1,0:T(8,128)} reduce(f32[32,2048,512]{2,1,0:T(8,128)} %all-gather.2.cloned.1.call-done, f32[]{:T(128)} %constant.290.clone.1), dimensions={0}, to_apply=%region_0.1 | reduce | flops 32505856 | bytes 138412032 | tf_op jit(solution)/shard_map/reduce_sum | solution.py:80
  764.0 11.7 cholesky.286
  788.3 11.7 cholesky.305
  811.8 11.7 cholesky.326
  834.8 11.7 cholesky.343
  856.3 68.4 %reshape.370 = f32[256,2,256,2]{3,2,1,0:T(8,128)} reshape(f32[512,512]{1,0:T(8,128)S(1)} %select_select_fusion.1) | data formatting | bytes 2097152 | tf_op jit(solution)/shard_map/reshape | solution.py:34
  924.7 35.9 %reshape.371 = f32[128,4,128,4]{3,2,1,0:T(8,128)} reshape(f32[512,512]{1,0:T(8,128)S(1)} %select_select_fusion.1) | data formatting | bytes 2097152 | tf_op jit(solution)/shard_map/reshape | solution.py:34
  985.1 107.3 %copy.213 = f32[256,2,256,2]{3,1,2,0:T(2,128)} copy(f32[256,2,256,2]{3,2,1,0:T(8,128)} %reshape.370) | data formatting | bytes 2097152 | tf_op jit(solution)/shard_map/reshape | solution.py:34
  1095.8 38.0 %copy.215 = f32[128,4,128,4]{3,1,2,0:T(4,128)} copy(f32[128,4,128,4]{3,2,1,0:T(8,128)} %reshape.371) | data formatting | bytes 2097152 | tf_op jit(solution)/shard_map/reshape | solution.py:34
  1138.0 20.5 %copy.217 = f32[64,8,64,8]{3,1,2,0:T(8,128)} copy(f32[64,8,64,8]{3,2,1,0:T(8,128)} %reshape.372) | data formatting | bytes 2097152 | tf_op jit(solution)/shard_map/reshape | solution.py:34
  1166.2 14.2 copy.219
  1215.6 127.5 %all-reduce.21.cloned.1.call-done = f32[512,512]{0,1:T(8,128)} async-done(((f32[512,512]{0,1:T(8,128)}), f32[512,512]{0,1:T(8,128)}) %all-reduce.21.cloned.1.call-update) | async-done | bytes 1048592 | tf_op jit(solution)/shard_map/psum | solution.py:90
  1345.1 11.7 cholesky.358
  1367.7 11.7 cholesky.377
  1389.9 11.7 cholesky.398
  1412.5 11.7 cholesky.415
  1434.5 68.4 %reshape.381 = f32[256,2,256,2]{3,2,1,0:T(8,128)} reshape(f32[512,512]{1,0:T(8,128)S(1)} %select_select_fusion) | data formatting | bytes 2097152 | tf_op jit(solution)/shard_map/reshape | solution.py:34
  1502.9 35.9 %reshape.382 = f32[128,4,128,4]{3,2,1,0:T(8,128)} reshape(f32[512,512]{1,0:T(8,128)S(1)} %select_select_fusion) | data formatting | bytes 2097152 | tf_op jit(solution)/shard_map/reshape | solution.py:34
  1563.6 107.3 %copy.212 = f32[256,2,256,2]{3,1,2,0:T(2,128)} copy(f32[256,2,256,2]{3,2,1,0:T(8,128)} %reshape.381) | data formatting | bytes 2097152 | tf_op jit(solution)/shard_map/reshape | solution.py:34
  1674.3 37.8 %copy.214 = f32[128,4,128,4]{3,1,2,0:T(4,128)} copy(f32[128,4,128,4]{3,2,1,0:T(8,128)} %reshape.382) | data formatting | bytes 2097152 | tf_op jit(solution)/shard_map/reshape | solution.py:34
  1716.3 20.3 %copy.216 = f32[64,8,64,8]{3,1,2,0:T(8,128)} copy(f32[64,8,64,8]{3,2,1,0:T(8,128)} %reshape.383) | data formatting | bytes 2097152 | tf_op jit(solution)/shard_map/reshape | solution.py:34
  1744.4 14.2 copy.218
  (247 shorter events, 262.2 us)
Async XLA Ops:
  7.2 701.9 %all-gather.2.cloned.1.call-start = ((), (), s32[]{:S(2)}) async-start(), calls=%async_computation | async-start | bytes 138412032 | tf_op jit(solution)/shard_map/all_gather | solution.py:80
  9.7 2.7 copy-start.22
  28.1 1315.0 %all-reduce.21.cloned.1.call-start = ((), (), s32[]{:S(2)}) async-start(), calls=%async_computation.1 | async-start | bytes 2097152 | tf_op jit(solution)/shard_map/psum | solution.py:90
  28.2 1105.6 %copy-start.4 = (s32[128]{0:T(128)}, s32[128]{0:T(128)S(1)}, u32[]{:S(2)}) copy-start(s32[128]{0:T(128)S(1)} %or_bitcast_fusion.6) | copy-start | bytes 1540
  31.5 1060.9 %copy-start.2 = (s32[256,1]{0,1:T(1,128)}, s32[256,1]{0,1:T(1,128)S(1)}, u32[]{:S(2)}) copy-start(s32[256,1]{0,1:T(1,128)S(1)} %shift-left_or_fusion.1) | copy-start | bytes 3076
  31.5 819.7 %copy-start = (s32[512,1]{0,1:T(1,128)}, s32[512,1]{0,1:T(1,128)S(1)}, u32[]{:S(2)}) copy-start(s32[512,1]{0,1:T(1,128)S(1)} %shift-left_or_fusion) | copy-start | bytes 6148
  1138.0 20.5 %copy-start.6 = (s32[64]{0:T(128)S(1)}, s32[64]{0:T(128)}, u32[]{:S(2)}) copy-start(s32[64]{0:T(128)} %or_bitcast_fusion.5) | copy-start | bytes 772
  1166.2 14.2 copy-start.15
  1185.3 5.5 copy-start.17
  1190.7 6.9 copy-start.20
  1197.7 4.2 copy-start.23
  1201.8 2.6 copy-start.25
  1210.5 1.4 copy-start.26
  1343.1 1.8 copy-start.8
  1345.1 84.5 %copy-start.1 = (s32[512,1]{0,1:T(1,128)S(1)}, s32[512,1]{0,1:T(1,128)}, u32[]{:S(2)}) copy-start(s32[512,1]{0,1:T(1,128)} %copy-done) | copy-start | bytes 6148
  1563.6 107.3 %copy-start.3 = (s32[256,1]{0,1:T(1,128)S(1)}, s32[256,1]{0,1:T(1,128)}, u32[]{:S(2)}) copy-start(s32[256,1]{0,1:T(1,128)} %copy-done.2) | copy-start | bytes 3076
  1674.3 37.8 %copy-start.5 = (s32[128]{0:T(128)S(1)}, s32[128]{0:T(128)}, u32[]{:S(2)}) copy-start(s32[128]{0:T(128)} %copy-done.4) | copy-start | bytes 1540
  1716.3 20.3 %copy-start.7 = (s32[64]{0:T(128)S(1)}, s32[64]{0:T(128)}, u32[]{:S(2)}) copy-start(s32[64]{0:T(128)} %or_bitcast_fusion.5) | copy-start | bytes 772
  1744.4 14.2 copy-start.16
  1763.4 5.5 copy-start.18
  1768.9 7.0 copy-start.21
  1775.9 6.7 copy-start.24
  1782.6 5.3 copy-start.9
  1788.0 1.7 copy-start.19
  (5 other events, 4.0 us)
Sparse Core Ops, SparseCore 0:
  28.2 680.7 all-gather.1
  1214.2 128.7 all-reduce.20
